TPU v7x, 512 devices: a whole 4x8x8 slice. The times are simulated.
512 devices in a mesh: chain: 2 (over x_lo), slab: 128 (over x_hi, z, y), vis: 2 (over core).
Axes of the slice: x: 4 (x_hi: 2, x_lo: 2; x = x_hi * 2 + x_lo), y: 8, z: 8, core: 2. Of those that a mesh axis runs over, the one named last changes fastest.
Arguments:
- screens: float32 [4, 2048, 2048], P(('chain', 'vis'), 'slab'), parts along dimension 0, may hold values from -6 to 6
- image: float32 [4096, 2048], P(('chain', 'slab')), parts along dimension 0, may hold values from -6 to 6
- vis_row: int32 [32768], P('slab'), may hold values from 0 to 2047
- vis_block: int32 [32768, 1], P('slab'), may hold values from 0 to 127; in each aligned block of 256 rows (0 to 255, 256 to 511, ...) at most 6 rows name the same one
- vis_column: int32 [32768], P('slab'), may hold values from 0 to 7
- vis_real: float32 [32768], P('slab'), may hold values from -6 to 6
- vis_imag: float32 [32768], P('slab'), may hold values from -6 to 6
- vis_weight: float32 [32768], P('slab'), may hold values from 0.5 to 4
Outputs:
- screen_grad: float32 [4, 2048, 2048], P(('chain', 'vis'), 'slab'), parts along dimension 0
There are 2 independent parts, one for each index of `chain`. A program takes and returns all parts, laid end to end along the dimension named above; an argument that names none is the same for every part. Nothing has to cross between parts.
Inputs may be any that keep to these rules, and one draw needn't show every extreme that they name: `vis_block`: among the 256 visibilities of one index of slab, at most 6 name any one block; in every draw some block of some index holds exactly 6.
All inputs are finite; a program needn't handle non-finite values.
Results may differ from a plain program's by a relative error of at most 0.013.
Values may be sent and summed in bfloat16 or wider, within the bound.
No kernel may reach another device: no remote copies, remote signals or barrier semaphores. Data moves between devices by JAX's collectives and lax.ppermute only.
A program may use at most 64 MiB of HBM per device.

v0:
```python
import math

import jax
import jax.numpy as jnp
from jax import lax
from jax.sharding import PartitionSpec as P

refract = 1.0
rank_rows = 512
sample_rows = 256
table_rows = 256


def with_halo(cells, sides, width):
    for axis, dim in sides:
        count = lax.axis_size(axis)
        head = lax.slice_in_dim(cells, 0, width, axis=dim)
        tail = lax.slice_in_dim(cells, cells.shape[dim] - width, cells.shape[dim], axis=dim)
        cells = jnp.concatenate(
            [
                lax.ppermute(tail, axis, [(i, (i + 1) % count) for i in range(count)]),
                cells,
                lax.ppermute(head, axis, [((i + 1) % count, i) for i in range(count)]),
            ],
            axis=dim,
        )
    return cells


def twiddle(first, second, length):
    phase = (first[:, None] * second[None, :] % length).astype(jnp.float32) * (
        2.0 * math.pi / length
    )
    return (jnp.cos(phase).astype(jnp.bfloat16), jnp.sin(phase).astype(jnp.bfloat16))


def col_slope(field):
    return (
        8.0 * (jnp.roll(field, -1, -1) - jnp.roll(field, 1, -1))
        - (jnp.roll(field, -2, -1) - jnp.roll(field, 2, -1))
    ) / 12.0


def col_adjoint(field):
    return (
        8.0 * (jnp.roll(field, 1, -1) - jnp.roll(field, -1, -1))
        - (jnp.roll(field, 2, -1) - jnp.roll(field, -2, -1))
    ) / 12.0


def row_slope(padded, row_count):
    return (
        8.0 * (padded[..., 3 : row_count + 3, :] - padded[..., 1 : row_count + 1, :])
        - (padded[..., 4 : row_count + 4, :] - padded[..., 0:row_count, :])
    ) / 12.0


def row_adjoint(padded, row_count):
    return (
        8.0 * (padded[..., 1 : row_count + 1, :] - padded[..., 3 : row_count + 3, :])
        - (padded[..., 0:row_count, :] - padded[..., 4 : row_count + 4, :])
    ) / 12.0


def local(screens, image, vis_row, vis_block, vis_column, vis_real, vis_imag, vis_weight):
    walkers, row_count, grid_size = screens.shape
    slabs = lax.axis_size("slab")
    half_kx = grid_size // 2
    vis_count = vis_row.shape[0]
    capacity = 3 * vis_count // slabs
    unitary = 1.0 / math.sqrt(grid_size)
    positions = jnp.arange(grid_size, dtype=jnp.int32)
    highest = lax.Precision.HIGHEST
    stacked = jnp.concatenate([screens, image[None]], axis=0)
    padded = with_halo(stacked.astype(jnp.bfloat16), (("slab", 1),), 2).astype(stacked.dtype)
    slope_x = col_slope(stacked)
    slope_y = row_slope(padded, row_count)
    joined = image[None] + refract * (
        slope_x[:walkers] * slope_x[walkers][None] + slope_y[:walkers] * slope_y[walkers][None]
    )
    joined_bf = joined.astype(jnp.bfloat16)
    owner_slab = vis_block[:, 0]
    owned = half_kx // slabs
    step_kx = min(table_rows, half_kx)
    real_parts = []
    imag_parts = []
    for offset in range(0, half_kx, step_kx):
        cos_rows, sin_rows = twiddle(
            offset + jnp.arange(step_kx, dtype=jnp.int32), positions, grid_size
        )
        with_cos = jnp.einsum(
            "kc,wrc->wkr", cos_rows, joined_bf, preferred_element_type=jnp.float32
        )
        with_sin = jnp.einsum(
            "kc,wrc->wkr", sin_rows, joined_bf, preferred_element_type=jnp.float32
        )
        real_parts.append((unitary * with_cos).astype(jnp.bfloat16))
        imag_parts.append((-unitary * with_sin).astype(jnp.bfloat16))
    spectra = jnp.stack([jnp.concatenate(real_parts, 1), jnp.concatenate(imag_parts, 1)])
    columns = lax.all_to_all(spectra, "slab", split_axis=2, concat_axis=3, tiled=True)
    payload = jnp.stack(
        [(vis_column * grid_size + vis_row).astype(jnp.float32), vis_real, vis_imag, vis_weight]
    )
    rank_size = math.gcd(rank_rows, vis_count)
    lower = (jnp.arange(rank_size)[:, None] > jnp.arange(rank_size)[None, :]).astype(jnp.float32)
    owner_hot = (owner_slab[:, None] == jnp.arange(slabs, dtype=jnp.int32)[None, :]).astype(
        jnp.float32
    )

    def rank_step(seen, hot_rows):
        before = jnp.dot(lower, hot_rows, precision=highest) + seen[None, :]
        return (seen + jnp.sum(hot_rows, 0), jnp.sum(before * hot_rows, 1))

    _, ranks = lax.scan(
        rank_step,
        jnp.zeros((slabs,), jnp.float32),
        owner_hot.reshape(vis_count // rank_size, rank_size, slabs),
    )
    destination = owner_slab * capacity + ranks.reshape(vis_count).astype(jnp.int32)
    buckets = (
        jnp.zeros((4, slabs * capacity), jnp.float32)
        .at[:, destination]
        .set(payload)
        .reshape(4, slabs, capacity)
    )
    arrived = lax.all_to_all(buckets, "slab", split_axis=1, concat_axis=1, tiled=True).reshape(
        4, slabs * capacity
    )
    span = walkers * owned
    flat = columns.reshape(2 * span, grid_size)
    total_slots = slabs * capacity
    step_rows = math.gcd(sample_rows, total_slots)
    owned_ids = jnp.arange(owned, dtype=jnp.int32)
    zeros_grid = jnp.zeros((span, grid_size), jnp.float32)

    def sample_step(index, sums):
        block_data = lax.dynamic_slice_in_dim(arrived, index * step_rows, step_rows, 1)
        cell_code = block_data[0].astype(jnp.int32)
        row_freq = cell_code % grid_size
        col_freq = cell_code // grid_size
        cos_rows, sin_rows = twiddle(row_freq, positions, grid_size)
        with_cos = lax.dot_general(
            cos_rows, flat, (((1,), (1,)), ((), ())), preferred_element_type=jnp.float32
        ).reshape(step_rows, 2, walkers, owned)
        with_sin = lax.dot_general(
            sin_rows, flat, (((1,), (1,)), ((), ())), preferred_element_type=jnp.float32
        ).reshape(step_rows, 2, walkers, owned)
        chooser = (col_freq[:, None] == owned_ids[None, :]).astype(jnp.float32)
        model_real = unitary * jnp.sum((with_cos[:, 0] + with_sin[:, 1]) * chooser[:, None, :], -1)
        model_imag = unitary * jnp.sum((with_cos[:, 1] - with_sin[:, 0]) * chooser[:, None, :], -1)
        error_real = (block_data[3][:, None] * (model_real - block_data[1][:, None])).astype(
            jnp.bfloat16
        )
        error_imag = (block_data[3][:, None] * (model_imag - block_data[2][:, None])).astype(
            jnp.bfloat16
        )
        spread = jnp.concatenate(
            [
                (error_real[:, :, None] * chooser[:, None, :]).reshape(step_rows, span),
                (error_imag[:, :, None] * chooser[:, None, :]).reshape(step_rows, span),
            ],
            1,
        ).astype(jnp.bfloat16)
        back_cos = lax.dot_general(
            spread, cos_rows, (((0,), (0,)), ((), ())), preferred_element_type=jnp.float32
        )
        back_sin = lax.dot_general(
            spread, sin_rows, (((0,), (0,)), ((), ())), preferred_element_type=jnp.float32
        )
        return (
            sums[0] + back_cos[:span] - back_sin[span:],
            sums[1] + back_sin[:span] + back_cos[span:],
        )

    sum_real, sum_imag = lax.fori_loop(
        0, total_slots // step_rows, sample_step, (zeros_grid, zeros_grid)
    )
    adjoint = (
        (unitary * jnp.stack([sum_real, sum_imag]))
        .astype(jnp.bfloat16)
        .reshape(2, walkers, owned, grid_size)
    )
    returned = lax.all_to_all(adjoint, "slab", split_axis=3, concat_axis=2, tiled=True)
    gradient = jnp.zeros((walkers, row_count, grid_size), jnp.float32)
    for offset in range(0, half_kx, step_kx):
        cos_rows, sin_rows = twiddle(
            offset + jnp.arange(step_kx, dtype=jnp.int32), positions, grid_size
        )
        part_real = returned[0][:, offset : offset + step_kx, :]
        part_imag = returned[1][:, offset : offset + step_kx, :]
        gradient = gradient + jnp.einsum(
            "wkr,kc->wrc", part_real, cos_rows, preferred_element_type=jnp.float32
        )
        gradient = gradient - jnp.einsum(
            "wkr,kc->wrc", part_imag, sin_rows, preferred_element_type=jnp.float32
        )
    gradient = unitary * gradient
    push_x = refract * slope_x[walkers][None] * gradient
    push_y = refract * slope_y[walkers][None] * gradient
    padded_y = with_halo(push_y.astype(jnp.bfloat16), (("slab", 1),), 2).astype(push_y.dtype)
    return col_adjoint(push_x) + row_adjoint(padded_y, row_count)


def solution(mesh):
    in_specs = (
        P(("chain", "vis"), "slab", None),
        P(("chain", "slab"), None),
        P("slab"),
        P("slab", None),
        P("slab"),
        P("slab"),
        P("slab"),
        P("slab"),
    )
    out_specs = P(("chain", "vis"), "slab", None)
    return jax.shard_map(local, mesh=mesh, in_specs=in_specs, out_specs=out_specs, check_vma=False)
```

profile of v0, /device:TPU:2, one launch (start us, length us, event | category | flops | bytes accessed | tf_op | source)
XLA Modules:
  0.0 358.0 jit_solution(11313475501157636354)
XLA Ops:
  4.5 13.8 %collective-permute-start.1 = (bf16[2,2,2048]{2,1,0:T(2,128)(2,1)S(1)}, bf16[2,2,2048]{2,1,0:T(2,128)(2,1)S(1)}, u32[]{:S(2)}, u32[]{:S(2)}) collective-permute-start(bf16[2,2,2048]{2,1,0:T(2,128)(2,1)S(1)} %get-tuple-element.290), channel_id=1, source_target_pairs={{2,0},{4,2},{6,4},{8,6},{10,8},{12,10},{14,12},{16,14},{18,16},{20... | collective-permute-start | bytes 49160 | tf_op jit(solution)/shard_map/ppermute | solution.py:23
  24.2 9.4 %all-to-all-start = ((f32[4,128,6]{2,0,1:T(4,128)}), f32[4,128,6]{2,0,1:T(4,128)S(1)}, u32[]{:S(2)}, u32[]{:S(2)}) async-start(f32[4,128,6]{2,0,1:T(4,128)} %copy.53), calls=%async_computation | async-start | bytes 524288 | tf_op jit(solution)/shard_map/all_to_all | solution.py:126
  34.5 8.8 %fusion.82 = bf16[1,256,16]{1,2,0:T(8,128)(2,1)S(1)} fusion(bf16[16,2048]{1,0:T(8,128)(2,1)S(1)} %fusion.111), kind=kOutput, calls=%fused_computation.142 | convolution fusion | flops 24649728 | bytes 73728 | tf_op jit(solution)/shard_map/kc,wrc->wkr/dot_general | solution.py:94
  43.3 8.1 %fusion.79 = bf16[1,256,16]{1,2,0:T(8,128)(2,1)S(1)} fusion(bf16[16,2048]{1,0:T(8,128)(2,1)S(1)} %fusion.111, s32[256]{0:T(256)S(1)} %iota_add_fusion), kind=kOutput, calls=%fused_computation.139 | convolution fusion | flops 24649728 | bytes 74752 | tf_op jit(solution)/shard_map/kc,wrc->wkr/dot_general | solution.py:94
  51.4 8.0 %fusion.83 = bf16[1,256,16]{1,2,0:T(8,128)(2,1)S(1)} fusion(bf16[16,2048]{1,0:T(8,128)(2,1)S(1)} %fusion.111, s32[256]{0:T(256)S(1)} %iota_add_fusion), kind=kOutput, calls=%fused_computation.143 | convolution fusion | flops 24649728 | bytes 74752 | tf_op jit(solution)/shard_map/kc,wrc->wkr/dot_general | solution.py:91
  59.4 8.6 %fusion.80 = bf16[1,256,16]{1,2,0:T(8,128)(2,1)S(1)} fusion(bf16[16,2048]{1,0:T(8,128)(2,1)S(1)} %fusion.111, s32[256]{0:T(256)S(1)} %iota_add_fusion.1), kind=kOutput, calls=%fused_computation.140 | convolution fusion | flops 24649728 | bytes 74752 | tf_op jit(solution)/shard_map/kc,wrc->wkr/dot_general | solution.py:94
  68.0 8.0 %fusion.84 = bf16[1,256,16]{1,2,0:T(8,128)(2,1)S(1)} fusion(bf16[16,2048]{1,0:T(8,128)(2,1)S(1)} %fusion.111, s32[256]{0:T(256)S(1)} %iota_add_fusion.1), kind=kOutput, calls=%fused_computation.144 | convolution fusion | flops 24649728 | bytes 74752 | tf_op jit(solution)/shard_map/kc,wrc->wkr/dot_general | solution.py:91
  76.0 8.3 %fusion.81 = bf16[1,256,16]{1,2,0:T(8,128)(2,1)S(1)} fusion(bf16[16,2048]{1,0:T(8,128)(2,1)S(1)} %fusion.111, s32[256]{0:T(256)S(1)} %iota_add_fusion.2), kind=kOutput, calls=%fused_computation.141 | convolution fusion | flops 24649728 | bytes 74752 | tf_op jit(solution)/shard_map/kc,wrc->wkr/dot_general | solution.py:94
  84.3 8.0 %fusion.85 = bf16[1,256,16]{1,2,0:T(8,128)(2,1)S(1)} fusion(bf16[16,2048]{1,0:T(8,128)(2,1)S(1)} %fusion.111, s32[256]{0:T(256)S(1)} %iota_add_fusion.2), kind=kOutput, calls=%fused_computation.145 | convolution fusion | flops 24649728 | bytes 74752 | tf_op jit(solution)/shard_map/kc,wrc->wkr/dot_general | solution.py:91
  92.3 8.7 %fusion.86 = bf16[1,256,16]{1,2,0:T(8,128)(2,1)S(1)} fusion(bf16[16,2048]{1,0:T(8,128)(2,1)S(1)} %fusion.111), kind=kOutput, calls=%fused_computation.146 | convolution fusion | flops 24649728 | bytes 73728 | tf_op jit(solution)/shard_map/kc,wrc->wkr/dot_general | solution.py:91
  102.5 16.4 %all-to-all-start.1 = ((bf16[128,2,128]{2,1,0:T(2,128)(2,1)}), bf16[128,2,128]{2,1,0:T(2,128)(2,1)S(1)}, u32[]{:S(2)}, u32[]{:S(2)}) async-start(bf16[128,2,128]{2,1,0:T(2,128)(2,1)} %reshape.696), calls=%async_computation.1 | async-start | bytes 131072 | tf_op jit(solution)/shard_map/all_to_all | solution.py:100
  119.1 14.2 %all-to-all-done.1 = bf16[128,2,128]{2,1,0:T(2,128)(2,1)S(1)} async-done(((bf16[128,2,128]{2,1,0:T(2,128)(2,1)}), bf16[128,2,128]{2,1,0:T(2,128)(2,1)S(1)}, u32[]{:S(2)}, u32[]{:S(2)}) %all-to-all-start.1) | async-done | bytes 65568 | tf_op jit(solution)/shard_map/all_to_all | solution.py:100
  134.6 120.4 %while.24 = (s32[]{:T(128)}, f32[8,2048]{1,0:T(8,128)S(1)}, f32[8,2048]{1,0:T(8,128)S(1)}, f32[4,768]{1,0:T(4,128)S(1)}, bf16[16,2048]{1,0:T(8,128)(2,1)S(1)}, /...) while((s32[]{:T(128)}, f32[8,2048]{1,0:T(8,128)S(1)}, ...), condition=%wide.region_5.6_spmd.clone.clone, body=%wide.region_2.5_spmd.clone.clone.sunk | while | flops 98724360 | bytes 1034473 | solution.py:175
  164.3 7.9 %fusion.212 = f32[256,16]{0,1:T(8,128)S(1)} fusion(bf16[16,2048]{1,0:T(8,128)(2,1)S(1)} %get-tuple-element.382, s32[256]{0:T(256)S(1)} %get-tuple-element.341), kind=kOutput, calls=%fused_computation.18.clone.1 | convolution fusion | flops 24641536 | bytes 82944 | tf_op jit(solution)/shard_map/while/body/eval_jaxpr/dot_general | solution.py:145
  196.0 7.9 %fusion.212 = f32[256,16]{0,1:T(8,128)S(1)} fusion(bf16[16,2048]{1,0:T(8,128)(2,1)S(1)} %get-tuple-element.382, s32[256]{0:T(256)S(1)} %get-tuple-element.341), kind=kOutput, calls=%fused_computation.18.clone.1 | convolution fusion | flops 24641536 | bytes 82944 | tf_op jit(solution)/shard_map/while/body/eval_jaxpr/dot_general | solution.py:145
  227.6 7.9 %fusion.212 = f32[256,16]{0,1:T(8,128)S(1)} fusion(bf16[16,2048]{1,0:T(8,128)(2,1)S(1)} %get-tuple-element.382, s32[256]{0:T(256)S(1)} %get-tuple-element.341), kind=kOutput, calls=%fused_computation.18.clone.1 | convolution fusion | flops 24641536 | bytes 82944 | tf_op jit(solution)/shard_map/while/body/eval_jaxpr/dot_general | solution.py:145
  256.9 20.0 %all_to_all.35 = bf16[128,2,128]{2,1,0:T(2,128)(2,1)S(1)} all-to-all(bf16[128,2,128]{2,1,0:T(2,128)(2,1)S(1)} %reshape.698), channel_id=1, replica_groups=mesh['chain'=2,'slab'=128,'vis'=2] {'slab'}, dimensions={0} | all-to-all | bytes 131072 | tf_op jit(solution)/shard_map/all_to_all | solution.py:183
  287.6 8.2 %convolution_subtract_fusion.3 = f32[16,2048]{1,0:T(8,128)S(1)} fusion(f32[16,2048]{1,0:T(8,128)S(1)} %fusion.87, bf16[1,1024,16]{2,1,0:T(8,128)(2,1)S(1)} %bitcast.172), kind=kOutput, calls=%fused_computation.88 | convolution fusion | flops 24674304 | bytes 327680 | tf_op jit(solution)/shard_map/wkr,kc->wrc/dot_general | solution.py:194
  295.8 8.0 %convolution_add_fusion.2 = f32[16,2048]{1,0:T(8,128)S(1)} fusion(f32[16,2048]{1,0:T(8,128)S(1)} %convolution_subtract_fusion.3, s32[256]{0:T(256)S(1)} %iota_add_fusion.2, bf16[1,1024,16]{2,1,0:T(8,128)(2,1)S(1)} %bitcast.177), kind=kOutput, calls=%fused_computation.87 | convolution fusion | flops 24674304 | bytes 328704 | tf_op jit(solution)/shard_map/wkr,kc->wrc/dot_general | solution.py:191
  303.7 7.9 %convolution_subtract_fusion.2 = f32[16,2048]{1,0:T(8,128)S(1)} fusion(f32[16,2048]{1,0:T(8,128)S(1)} %convolution_add_fusion.2, s32[256]{0:T(256)S(1)} %iota_add_fusion.2, bf16[1,1024,16]{2,1,0:T(8,128)(2,1)S(1)} %bitcast.173), kind=kOutput, calls=%fused_computation.86 | convolution fusion | flops 24674304 | bytes 328704 | tf_op jit(solution)/shard_map/wkr,kc->wrc/dot_general | solution.py:194
  311.6 8.0 %convolution_add_fusion.1 = f32[16,2048]{1,0:T(8,128)S(1)} fusion(f32[16,2048]{1,0:T(8,128)S(1)} %convolution_subtract_fusion.2, s32[256]{0:T(256)S(1)} %iota_add_fusion.1, bf16[1,1024,16]{2,1,0:T(8,128)(2,1)S(1)} %bitcast.178), kind=kOutput, calls=%fused_computation.85 | convolution fusion | flops 24674304 | bytes 328704 | tf_op jit(solution)/shard_map/wkr,kc->wrc/dot_general | solution.py:191
  319.6 8.3 %convolution_subtract_fusion.1 = f32[16,2048]{1,0:T(8,128)S(1)} fusion(f32[16,2048]{1,0:T(8,128)S(1)} %convolution_add_fusion.1, s32[256]{0:T(256)S(1)} %iota_add_fusion.1, bf16[1,1024,16]{2,1,0:T(8,128)(2,1)S(1)} %bitcast.174), kind=kOutput, calls=%fused_computation.84 | convolution fusion | flops 24674304 | bytes 328704 | tf_op jit(solution)/shard_map/wkr,kc->wrc/dot_general | solution.py:194
  335.7 8.1 %slice_multiply_fusion.2 = (f32[1,16,2048]{2,1,0:T(8,128)S(1)}, bf16[1,16,2048]{2,1,0:T(8,128)(2,1)S(1)}) fusion(f32[2,16,2048]{2,1,0:T(8,128)S(1)} %fusion.98, f32[2,16,2048]{2,1,0:T(8,128)S(1)} %fusion.94, f32[16,2048]{1,0:T(8,128)S(1)} %convolution_add_fusion, s32[256]{0:T(256)S(1)} %iota_add_fusion, bf16[1,1024,16]{2,1,0:T(8,128)(2,1)S(1)} %bitcast.175), kind=kOutput, calls=%fused_computation.206 | convolution fusion | flops 24805376 | bytes 656384 | tf_op jit(solution)/shard_map/wkr,kc->wrc/dot_general | solution.py:194
  346.6 9.0 %collective-permute-start.3 = (bf16[1,2,2048]{2,1,0:T(2,128)(2,1)S(1)}, bf16[1,2,2048]{2,1,0:T(2,128)(2,1)S(1)}, u32[]{:S(2)}, u32[]{:S(2)}) collective-permute-start(bf16[1,2,2048]{2,1,0:T(2,128)(2,1)S(1)} %get-tuple-element.292), channel_id=1, source_target_pairs={{2,0},{4,2},{6,4},{8,6},{10,8},{12,10},{14,12},{16,14},{18,16},{20... | collective-permute-start | bytes 24584 | tf_op jit(solution)/shard_map/ppermute | solution.py:23
  (90 shorter events, 110.4 us)
Async XLA Ops:
  1.0 33.2 %collective-permute-start = (bf16[2,2,2048]{2,1,0:T(2,128)(2,1)S(1)}, bf16[2,2,2048]{2,1,0:T(2,128)(2,1)S(1)}, u32[]{:S(2)}, u32[]{:S(2)}) collective-permute-start(bf16[2,2,2048]{2,1,0:T(2,128)(2,1)S(1)} %get-tuple-element.289), channel_id=1, source_target_pairs={{0,2},{2,4},{4,6},{6,8},{8,10},{10,12},{12,14},{14,16},{16,18},{18... | collective-permute-start | bytes 49160 | tf_op jit(solution)/shard_map/ppermute | solution.py:21
  4.5 29.8 %collective-permute-start.1 = (bf16[2,2,2048]{2,1,0:T(2,128)(2,1)S(1)}, bf16[2,2,2048]{2,1,0:T(2,128)(2,1)S(1)}, u32[]{:S(2)}, u32[]{:S(2)}) collective-permute-start(bf16[2,2,2048]{2,1,0:T(2,128)(2,1)S(1)} %get-tuple-element.290), channel_id=1, source_target_pairs={{2,0},{4,2},{6,4},{8,6},{10,8},{12,10},{14,12},{16,14},{18,16},{20... | collective-permute-start | bytes 49160 | tf_op jit(solution)/shard_map/ppermute | solution.py:23
  21.6 11.9 %copy-start = (f32[16,2048]{1,0:T(8,128)S(1)}, f32[16,2048]{1,0:T(8,128)}, u32[]{:S(2)}) copy-start(f32[16,2048]{1,0:T(8,128)} %param.11) | copy-start | bytes 393220
  21.6 11.9 %copy-start.1 = (f32[1,16,2048]{2,1,0:T(8,128)S(1)}, f32[1,16,2048]{2,1,0:T(8,128)}, u32[]{:S(2)}) copy-start(f32[1,16,2048]{2,1,0:T(8,128)} %param.10) | copy-start | bytes 393220
  24.2 78.3 %all-to-all-start = ((f32[4,128,6]{2,0,1:T(4,128)}), f32[4,128,6]{2,0,1:T(4,128)S(1)}, u32[]{:S(2)}, u32[]{:S(2)}) async-start(f32[4,128,6]{2,0,1:T(4,128)} %copy.53), calls=%async_computation | async-start | bytes 524288 | tf_op jit(solution)/shard_map/all_to_all | solution.py:126
  102.5 30.8 %all-to-all-start.1 = ((bf16[128,2,128]{2,1,0:T(2,128)(2,1)}), bf16[128,2,128]{2,1,0:T(2,128)(2,1)S(1)}, u32[]{:S(2)}, u32[]{:S(2)}) async-start(bf16[128,2,128]{2,1,0:T(2,128)(2,1)} %reshape.696), calls=%async_computation.1 | async-start | bytes 131072 | tf_op jit(solution)/shard_map/all_to_all | solution.py:100
  344.1 11.7 %collective-permute-start.2 = (bf16[1,2,2048]{2,1,0:T(2,128)(2,1)S(1)}, bf16[1,2,2048]{2,1,0:T(2,128)(2,1)S(1)}, u32[]{:S(2)}, u32[]{:S(2)}) collective-permute-start(bf16[1,2,2048]{2,1,0:T(2,128)(2,1)S(1)} %get-tuple-element.291), channel_id=1, source_target_pairs={{0,2},{2,4},{4,6},{6,8},{8,10},{10,12},{12,14},{14,16},{16,18},{18... | collective-permute-start | bytes 24584 | tf_op jit(solution)/shard_map/ppermute | solution.py:21
  346.6 10.4 %collective-permute-start.3 = (bf16[1,2,2048]{2,1,0:T(2,128)(2,1)S(1)}, bf16[1,2,2048]{2,1,0:T(2,128)(2,1)S(1)}, u32[]{:S(2)}, u32[]{:S(2)}) collective-permute-start(bf16[1,2,2048]{2,1,0:T(2,128)(2,1)S(1)} %get-tuple-element.292), channel_id=1, source_target_pairs={{2,0},{4,2},{6,4},{8,6},{10,8},{12,10},{14,12},{16,14},{18,16},{20... | collective-permute-start | bytes 24584 | tf_op jit(solution)/shard_map/ppermute | solution.py:23
where the time goes:
time: 361 us; the launch traced here: 358 us
  matrix products  226 us (63%)
  starting transfers between devices  54.7 us (15%)
  loops' own time  25.6 us (7%)
  blocking collectives  20 us (6%)
  waiting for transfers between devices  15.4 us (4%)
  local copies, waits for them, and re-layouts  10.7 us (3%)
  other arithmetic  5.4 us (1%)
    dot_general x4, matrix products, local(): jnp.einsum('kc,wrc->wkr', sin_rows, joined_bf, preferred_element_type=jnp...  33.7 us
    dot_general x4, matrix products, local(): jnp.einsum('kc,wrc->wkr', cos_rows, joined_bf, preferred_element_type=jnp...  32.8 us
    dot_general x4, matrix products, local(): jnp.einsum('wkr,kc->wrc', part_imag, sin_rows, preferred_element_type=jnp...  32.4 us
    dot_general x4, matrix products, local(): jnp.einsum('wkr,kc->wrc', part_real, cos_rows, preferred_element_type=jnp...  31.5 us
    another operation x1, loops' own time, local(): lax.fori_loop(0, total_slots // step_rows, sample_step, (zeros_grid, zero...  25.6 us
    dot_general x3, matrix products, sample_step(): lax.dot_general(sin_rows, flat, (((1,), (1,)), ((), ())), preferred_eleme...  23.8 us
    dot_general x3, matrix products, sample_step(): lax.dot_general(spread, sin_rows, (((0,), (0,)), ((), ())), preferred_ele...  23.6 us
    dot_general x3, matrix products, sample_step(): lax.dot_general(cos_rows, flat, (((1,), (1,)), ((), ())), preferred_eleme...  23.5 us
  transfers between devices with their start and end apart: 6, of which 2 were waited for; matrix products, arithmetic and copies ran while one was open for 21% of the time, Pallas kernels for 0%

commit v1 on v0

v1 whole, which is shorter than its diff:
```python
import functools
import math

import jax
import jax.numpy as jnp
import numpy as np
from jax import lax
from jax.experimental import pallas as pl
from jax.experimental.pallas import tpu as pltpu
from jax.sharding import PartitionSpec as P

INTERPRET = False
F32 = jnp.float32
BF16 = jnp.bfloat16

GRID = 2048
ROWS = 16
SLABS = 128
OWNED = 8
CAP = 6
SLOTS = 8
FIELDS = 8
UNITARY = 1.0 / math.sqrt(GRID)
NT = (((1,), (1,)), ((), ()))


def wave(first, second, length):
    phase = (np.arange(first)[:, None] * np.arange(second)[None, :] % length) * (2.0 * np.pi / length)
    return np.cos(phase), np.sin(phase)


@functools.lru_cache(None)
def tables():
    out = {}
    cos, sin = wave(64, 128, 128)
    wide = np.zeros((2, 64, 2, 2, 2, 128))
    for half in range(2):
        wide[0, :, half, half, 0] = cos
        wide[0, :, half, half, 1] = sin
        wide[1, :, half, half, 0] = -sin
        wide[1, :, half, half, 1] = cos
    out["row_mix"] = (UNITARY * wide.reshape(256, 512), BF16)
    cos, sin = wave(16, 128, GRID)
    out["row_turn"] = (np.concatenate([cos, sin], 0), F32)
    cos, sin = wave(128, 128, 128)
    mix = UNITARY * np.block([[cos, sin], [-sin, cos]])
    out["col_mix"] = (mix, BF16)
    out["col_mix_back"] = (mix.T, BF16)
    cos, sin = wave(128, 16, GRID)
    out["col_turn"] = (np.concatenate([np.tile(cos, (1, 8)), np.tile(sin, (1, 8))], 1), F32)
    cos, sin = wave(16, 16, 16)
    cos, sin = np.kron(np.eye(8), cos), np.kron(np.eye(8), sin)
    mix = np.block([[cos, -sin], [sin, cos]])
    out["fine_mix"] = (mix, BF16)
    out["fine_mix_back"] = (mix.T, BF16)
    cos, sin = wave(256, 128, 256)
    out["out_mix"] = (UNITARY * np.block([[cos, -sin], [sin, cos]]), BF16)
    cos, sin = wave(256, 8, GRID)
    out["out_turn"] = (np.concatenate([np.repeat(cos, 16, 1), np.repeat(sin, 16, 1)], 1), F32)
    cos, sin = wave(8, 8, 8)
    out["out_fine"] = (np.concatenate([np.kron(cos, np.eye(16)), -np.kron(sin, np.eye(16))], 1), BF16)
    return out


def table(name):
    values, kind = tables()[name]
    return jnp.asarray(values.astype(np.float32)).astype(kind)


def roll(field, shift, axis):
    return pltpu.roll(field, shift % field.shape[axis], axis)


def col_slope(field):
    return (8.0 / 12.0) * (roll(field, -1, 1) - roll(field, 1, 1)) - (1.0 / 12.0) * (
        roll(field, -2, 1) - roll(field, 2, 1)
    )


def row_slope(ref, count):
    return (8.0 / 12.0) * (ref[3 : count + 3, :] - ref[1 : count + 1, :]) - (1.0 / 12.0) * (
        ref[4 : count + 4, :] - ref[0:count, :]
    )


def bucket_kernel(cells, bucket):
    data = cells[...]
    count = data.shape[1]
    block = data[1:2, :]
    hot = (lax.broadcasted_iota(jnp.int32, (SLABS, count), 0).astype(F32) == block).astype(F32)
    earlier = (
        lax.broadcasted_iota(jnp.int32, (count, count), 0)
        < lax.broadcasted_iota(jnp.int32, (count, count), 1)
    ).astype(F32).astype(BF16)
    before = jnp.dot(hot.astype(BF16), earlier, preferred_element_type=F32)
    rank = jnp.sum(before * hot, 0, keepdims=True)
    row = data[0:1, :]
    row_high = jnp.floor(row * (1.0 / 128.0))
    weight = data[5:6, :]
    fields = [row - 128.0 * row_high, data[2:3, :] * 16.0 + row_high]
    for value in (weight, weight * data[3:4, :], weight * data[4:5, :]):
        high = value.astype(BF16).astype(F32)
        fields += [high, value - high]
    slot = lax.broadcasted_iota(jnp.int32, (SLOTS, count), 0).astype(F32)
    mine = slot == rank
    spread = jnp.concatenate([jnp.where(mine, field, 0.0) for field in fields], 0)
    filled = lax.dot_general(hot.astype(BF16), spread.astype(BF16), NT, preferred_element_type=F32)
    bucket[...] = jnp.concatenate([filled, jnp.zeros_like(filled)], 1)


def forward_kernel(screen, image, above, below, bucket, mix, turn, message, image_x, image_y, pad_image, pad_screen, mixed):
    top = above[...].astype(F32)
    low = below[...].astype(F32)
    own_screen = screen[0]
    own_image = image[...]
    pad_image[0:4, :] = top[0:4]
    pad_image[4:20, :] = own_image
    pad_image[20:24, :] = low[0:4]
    pad_screen[0:2, :] = top[4:6]
    pad_screen[2:18, :] = own_screen
    pad_screen[18:20, :] = low[4:6]
    image_y[0:20, :] = row_slope(pad_image, 20)
    slope_x = col_slope(own_image)
    image_x[...] = slope_x
    joined = own_image + col_slope(own_screen) * slope_x + row_slope(pad_screen, 16) * image_y[2:18, :]
    joined = joined.astype(BF16).astype(F32)
    part = [joined[:, 128 * i : 128 * (i + 1)] for i in range(16)]
    even = [part[i] + part[16 - i] for i in range(1, 8)]
    odd = [part[i] - part[16 - i] for i in range(1, 8)]
    for k in range(9):
        real = part[0] + part[8] if k % 2 == 0 else part[0] - part[8]
        imag = jnp.zeros_like(real)
        for i in range(1, 8):
            angle = 2.0 * math.pi * ((i * k) % 16) / 16.0
            real = real + math.cos(angle) * even[i - 1]
            if (i * k) % 8 != 0:
                imag = imag - math.sin(angle) * odd[i - 1]
        for target in {k, (16 - k) % 16}:
            sign = 1.0 if target == k else -1.0
            cos = turn[target : target + 1, :]
            sin = turn[16 + target : 17 + target, :]
            half, fine = divmod(target, 8)
            rows = slice(16 * fine, 16 * fine + 16)
            mixed[rows, 256 * half : 256 * half + 128] = (real * cos + (sign * imag) * sin).astype(BF16)
            mixed[rows, 256 * half + 128 : 256 * half + 256] = ((sign * imag) * cos - real * sin).astype(BF16)
    spectra = lax.dot_general(mix[...], mixed[...], NT, preferred_element_type=F32)
    message[:, 0, :] = spectra[0:128]
    message[:, 1, :] = spectra[128:256]
    message[:, 2, :] = bucket[...]


def middle_kernel(arrived, mix, turn, fine, fine_back, mix_back, message):
    cells = jnp.transpose(arrived[:, 2, :])
    total = SLABS * CAP
    index = lax.broadcasted_iota(jnp.int32, (128, total), 0).astype(F32)

    def line(field):
        return jnp.concatenate([cells[SLOTS * field + s : SLOTS * field + s + 1, :] for s in range(CAP)], 1)

    row_hot = (index == line(0)).astype(F32).astype(BF16)
    chosen = index == line(1)
    spread = jnp.concatenate(
        [jnp.where(chosen, line(2 + t), 0.0).astype(BF16) for t in range(6)], 0
    )
    sums = lax.dot_general(row_hot, spread, NT, preferred_element_type=F32)
    weight = sums[:, 0:128] + sums[:, 128:256]
    seen_real = sums[:, 256:384] + sums[:, 384:512]
    seen_imag = sums[:, 512:640] + sums[:, 640:768]
    cos = turn[:, 0:128]
    sin = turn[:, 128:256]
    spectra = jnp.concatenate([arrived[:, 0, :], arrived[:, 1, :]], 0).astype(BF16)
    coarse = jnp.dot(mix[...], spectra, preferred_element_type=F32)
    real, imag = coarse[0:128], coarse[128:256]
    turned = jnp.concatenate([real * cos + imag * sin, imag * cos - real * sin], 1).astype(BF16)
    model = jnp.dot(turned, fine[...], preferred_element_type=F32)
    error = jnp.concatenate(
        [weight * model[:, 0:128] - seen_real, weight * model[:, 128:256] - seen_imag], 1
    ).astype(BF16)
    spread_back = jnp.dot(error, fine_back[...], preferred_element_type=F32)
    real, imag = spread_back[:, 0:128], spread_back[:, 128:256]
    turned = jnp.concatenate([real * cos - imag * sin, imag * cos + real * sin], 0).astype(BF16)
    back = jnp.dot(mix_back[...], turned, preferred_element_type=F32)
    back_real, back_imag = back[0:128], back[128:256]
    row = lax.broadcasted_iota(jnp.int32, (128, 128), 1) % ROWS
    first = row < 2
    real_side = jnp.where(first, roll(back_real, -1, 0), roll(back_real, 1, 0))
    imag_side = jnp.where(first, roll(back_imag, -1, 0), roll(back_imag, 1, 0))
    message[:, 0, :] = back_real
    message[:, 1, :] = back_imag
    message[:, 2, :] = jnp.where(first | (row >= ROWS - 2), real_side, roll(imag_side, 8, 1))


def final_kernel(arrived, image_x, image_y, mix, turn, fine, out, push):
    side = arrived[:, 2, :]
    adjoint = jnp.concatenate(
        [
            jnp.concatenate([arrived[:, 0, :], side], 1),
            jnp.concatenate([arrived[:, 1, :], roll(side, -8, 1)], 1),
        ],
        0,
    ).astype(BF16)
    coarse = jnp.dot(mix[...], adjoint, preferred_element_type=F32)
    cos = turn[:, 0:128]
    sin = turn[:, 128:256]
    grads = []
    for lanes in (slice(0, 128), slice(128, 256)):
        real, imag = coarse[0:256, lanes], coarse[256:512, lanes]
        turned = jnp.concatenate([real * cos - imag * sin, real * sin + imag * cos], 1).astype(BF16)
        flat = lax.dot_general(fine[...], turned, NT, preferred_element_type=F32)
        grads.append(jnp.concatenate([flat[16 * i : 16 * i + 16, :] for i in range(8)], 1))
    own, near = grads
    push[0:2, :] = image_y[0:2, :] * near[14:16]
    push[2:18, :] = image_y[2:18, :] * own
    push[18:20, :] = image_y[18:20, :] * near[0:2]
    out[0] = -(col_slope(image_x[...] * own) + row_slope(push, ROWS))


def call(kernel, out_shape, scratch, *args):
    return pl.pallas_call(
        kernel,
        out_shape=out_shape,
        scratch_shapes=scratch,
        interpret=INTERPRET,
    )(*args)


def local(screens, image, vis_row, vis_block, vis_column, vis_real, vis_imag, vis_weight):
    shape = jax.ShapeDtypeStruct
    onward = [(i, (i + 1) % SLABS) for i in range(SLABS)]
    backward = [((i + 1) % SLABS, i) for i in range(SLABS)]
    fill = jnp.zeros((2, GRID), BF16)
    tail = jnp.concatenate([image[12:16].astype(BF16), screens[0, 14:16].astype(BF16), fill], 0)
    head = jnp.concatenate([image[0:4].astype(BF16), screens[0, 0:2].astype(BF16), fill], 0)
    above = lax.ppermute(tail, "slab", onward)
    below = lax.ppermute(head, "slab", backward)
    cells = jnp.stack(
        [
            vis_row.astype(F32),
            vis_block[:, 0].astype(F32),
            vis_column.astype(F32),
            vis_real,
            vis_imag,
            vis_weight,
            jnp.zeros_like(vis_real),
            jnp.zeros_like(vis_real),
        ]
    )
    bucket = call(bucket_kernel, shape((SLABS, 128), F32), [], cells)
    message, image_x, image_y = call(
        forward_kernel,
        (shape((SLABS, 3, 128), F32), shape((ROWS, GRID), F32), shape((24, GRID), F32)),
        [pltpu.VMEM((24, GRID), F32), pltpu.VMEM((24, GRID), F32), pltpu.VMEM((128, 512), BF16)],
        screens, image, above, below, bucket, table("row_mix"), table("row_turn"),
    )
    arrived = lax.all_to_all(message, "slab", 0, 0, tiled=True)
    message = call(
        middle_kernel, shape((SLABS, 3, 128), F32), [],
        arrived, table("col_mix"), table("col_turn"), table("fine_mix"), table("fine_mix_back"), table("col_mix_back"),
    )
    arrived = lax.all_to_all(message, "slab", 0, 0, tiled=True)
    return call(
        final_kernel, shape((1, ROWS, GRID), F32), [pltpu.VMEM((24, GRID), F32)],
        arrived, image_x, image_y, table("out_mix"), table("out_turn"), table("out_fine"),
    )


def solution(mesh):
    in_specs = (
        P(("chain", "vis"), "slab", None),
        P(("chain", "slab"), None),
        P("slab"),
        P("slab", None),
        P("slab"),
        P("slab"),
        P("slab"),
        P("slab"),
    )
    out_specs = P(("chain", "vis"), "slab", None)
    return jax.shard_map(local, mesh=mesh, in_specs=in_specs, out_specs=out_specs, check_vma=False)
```

time: 361 us -> 84.1 us (0.23)
  the two profiles are of different devices: /device:TPU:2 before, /device:TPU:8 now
where the time goes in v1:
time: 84.1 us; the launch traced here: 83.6 us
  blocking collectives  53.1 us (63%)
  Pallas kernels  9.82 us (12%)
  starting transfers between devices  9.62 us (11%)
  waiting for transfers between devices  7.2 us (9%)
  local copies, waits for them, and re-layouts  2.71 us (3%)
  other arithmetic  1.05 us (1%)
    all_to_all x2, blocking collectives, local(): arrived = lax.all_to_all(message, 'slab', 0, 0, tiled=True)  53.1 us
    pallas_call x4, Pallas kernels, call(): pl.pallas_call(kernel, out_shape=out_shape, scratch_shapes=scratch, inter...  9.82 us
    ppermute x1, starting transfers between devices, local(): below = lax.ppermute(head, 'slab', backward)  7.7 us
    ppermute x1, waiting for transfers between devices, local(): above = lax.ppermute(tail, 'slab', onward)  7.2 us
    unnamed x18, local copies, waits for them, and re-layouts  1.98 us
    ppermute x1, starting transfers between devices, local(): above = lax.ppermute(tail, 'slab', onward)  1.92 us
  transfers between devices with their start and end apart: 2, of which 1 were waited for; matrix products, arithmetic and copies ran while one was open for 1% of the time, Pallas kernels for 2%

profile of v1, /device:TPU:8, one launch (start us, length us, event | category | flops | bytes accessed | tf_op | source)
XLA Modules:
  0.0 83.6 jit_solution(2001536554583943281)
XLA Ops:
  0.0 0.9 %convert.9 = bf16[1,16,2048]{2,1,0:T(8,128)(2,1)S(1)} convert(f32[1,16,2048]{2,1,0:T(8,128)} %screen.1) | non-fusion elementwise | flops 32768 | bytes 196608 | tf_op jit(solution)/shard_map/convert.2
  1.0 0.0 copy-done
  1.0 0.1 pad.5.clone
  1.1 0.1 maximum_maximum_fusion.1
  1.2 7.7 %collective-permute-start.1 = (bf16[8,2048]{1,0:T(8,128)(2,1)S(1)}, bf16[8,2048]{1,0:T(8,128)(2,1)S(1)}, u32[]{:S(2)}, u32[]{:S(2)}) collective-permute-start(bf16[8,2048]{1,0:T(8,128)(2,1)S(1)} %get-tuple-element.15), channel_id=1, source_target_pairs={{2,0},{4,2},{6,4},{8,6},{10,8},{12,10},{14,12},{16,14},{18,16},{20... | collective-permute-start | bytes 98312 | tf_op jit(solution)/shard_map/ppermute | solution.py:235
  8.9 0.0 copy-start.7
  8.9 1.9 %collective-permute-start = (bf16[8,2048]{1,0:T(8,128)(2,1)S(1)}, bf16[8,2048]{1,0:T(8,128)(2,1)S(1)}, u32[]{:S(2)}, u32[]{:S(2)}) collective-permute-start(bf16[8,2048]{1,0:T(8,128)(2,1)S(1)} %get-tuple-element.16), channel_id=1, source_target_pairs={{0,2},{2,4},{4,6},{6,8},{8,10},{10,12},{12,14},{14,16},{16,18},{18... | collective-permute-start | bytes 98312 | tf_op jit(solution)/shard_map/ppermute | solution.py:234
  10.9 0.0 copy-done.6
  10.9 0.0 copy-done.7
  10.9 0.0 copy-start.8
  10.9 0.7 copy-done.8
  11.6 0.7 copy-done.5
  12.2 0.0 copy-done.3
  12.3 0.0 copy-done.4
  12.3 0.6 stack.28.cells
  12.9 1.7 %shard_map.172.bucket = f32[128,128]{1,0:T(8,128)} custom-call(f32[8,256]{1,0:T(8,128)} %stack.28.cells), custom_call_target="tpu_custom_call" | custom-call | tf_op jit(solution)/shard_map/pallas_call | solution.py:219
  14.6 0.0 collective-permute-done.1.below
  14.6 7.2 %collective-permute-done.above = bf16[8,2048]{1,0:T(8,128)(2,1)S(1)} collective-permute-done((bf16[8,2048]{1,0:T(8,128)(2,1)S(1)}, bf16[8,2048]{1,0:T(8,128)(2,1)S(1)}, u32[]{:S(2)}, u32[]{:S(2)}) %collective-permute-start) | collective-permute-done | bytes 32800 | tf_op jit(solution)/shard_map/ppermute | solution.py:234
  21.8 0.6 copy-done.2
  22.4 2.5 %shard_map.173 = (f32[128,3,128]{2,1,0:T(4,128)}, f32[16,2048]{1,0:T(8,128)}, f32[24,2048]{1,0:T(8,128)}) custom-call(f32[1,16,2048]{2,1,0:T(8,128)} %screen.1, f32[16,2048]{1,0:T(8,128)} %image.1, bf16[8,2048]{1,0:T(8,128)(2,1)} %copy-done.2, bf16[8,2048]{1,0:T(8,128)(2,1)} %copy-done.1, f32[128,128]{1,0:T(8,128)} %shard_map.172.bucket, ...), custom_call_target="tpu_custom_call" | custom-call | tf_op jit(solution)/shard_map/pallas_call | solution.py:219
  24.9 29.9 %all_to_all.10.arrived = f32[128,3,128]{2,1,0:T(4,128)} all-to-all(f32[128,3,128]{2,1,0:T(4,128)} %get-tuple-element.8), channel_id=1, replica_groups=mesh['chain'=2,'slab'=128,'vis'=2] {'slab'}, dimensions={0} | all-to-all | bytes 393216 | tf_op jit(solution)/shard_map/all_to_all | solution.py:255
  54.8 3.0 %shard_map.174 = f32[128,3,128]{2,1,0:T(4,128)} custom-call(f32[128,3,128]{2,1,0:T(4,128)} %all_to_all.10.arrived, bf16[256,256]{1,0:T(8,128)(2,1)} %constant.37.mix, f32[128,256]{1,0:T(8,128)} %constant.27.clone.turn, bf16[256,256]{1,0:T(8,128)(2,1)} %constant.38.fine, bf16[256,256]{1,0:T(8,128)(2,1)} %constant.39.fine_back, bf16[256,256]{1,0:T(8,128)(2,1)} %constant.40.mix_back), custom_call_target="tpu_custom_call" | custom-call | tf_op jit(solution)/shard_map/pallas_call | solution.py:219
  57.9 23.2 %all_to_all.11.arrived = f32[128,3,128]{2,1,0:T(4,128)} all-to-all(f32[128,3,128]{2,1,0:T(4,128)} %shard_map.174), channel_id=1, replica_groups=mesh['chain'=2,'slab'=128,'vis'=2] {'slab'}, dimensions={0} | all-to-all | bytes 393216 | tf_op jit(solution)/shard_map/all_to_all | solution.py:260
  81.0 2.6 %shard_map.175 = f32[1,16,2048]{2,1,0:T(8,128)} custom-call(f32[128,3,128]{2,1,0:T(4,128)} %all_to_all.11.arrived, f32[16,2048]{1,0:T(8,128)} %get-tuple-element.9.image_x, f32[24,2048]{1,0:T(8,128)} %get-tuple-element.10.image_y, bf16[512,256]{1,0:T(8,128)(2,1)} %constant.41.mix, f32[256,256]{1,0:T(8,128)} %constant.32.clone.turn, ...), custom_call_target="tpu_custom_call" | custom-call | tf_op jit(solution)/shard_map/pallas_call | solution.py:219
  (16 shorter events, 0.1 us)
Async XLA Ops:
  0.0 1.0 %copy-start = (f32[16,2048]{1,0:T(8,128)S(1)}, f32[16,2048]{1,0:T(8,128)}, u32[]{:S(2)}) copy-start(f32[16,2048]{1,0:T(8,128)} %image.1) | copy-start | bytes 393220
  1.2 9.7 %copy-start.6 = (s32[256,1]{0,1:T(1,128)S(1)}, s32[256,1]{0,1:T(1,128)}, u32[]{:S(2)}) copy-start(s32[256,1]{0,1:T(1,128)} %param.21) | copy-start | bytes 3076
  1.2 13.4 %collective-permute-start.1 = (bf16[8,2048]{1,0:T(8,128)(2,1)S(1)}, bf16[8,2048]{1,0:T(8,128)(2,1)S(1)}, u32[]{:S(2)}, u32[]{:S(2)}) collective-permute-start(bf16[8,2048]{1,0:T(8,128)(2,1)S(1)} %get-tuple-element.15), channel_id=1, source_target_pairs={{2,0},{4,2},{6,4},{8,6},{10,8},{12,10},{14,12},{16,14},{18,16},{20... | collective-permute-start | bytes 98312 | tf_op jit(solution)/shard_map/ppermute | solution.py:235
  8.9 2.0 %copy-start.7 = (s32[256]{0:T(256)S(1)}, s32[256]{0:T(256)}, u32[]{:S(2)}) copy-start(s32[256]{0:T(256)} %param.20) | copy-start | bytes 3076
  8.9 12.9 %collective-permute-start = (bf16[8,2048]{1,0:T(8,128)(2,1)S(1)}, bf16[8,2048]{1,0:T(8,128)(2,1)S(1)}, u32[]{:S(2)}, u32[]{:S(2)}) collective-permute-start(bf16[8,2048]{1,0:T(8,128)(2,1)S(1)} %get-tuple-element.16), channel_id=1, source_target_pairs={{0,2},{2,4},{4,6},{6,8},{8,10},{10,12},{12,14},{14,16},{16,18},{18... | collective-permute-start | bytes 98312 | tf_op jit(solution)/shard_map/ppermute | solution.py:234
  10.9 0.7 copy-start.8
  11.6 0.7 copy-start.5
  11.6 0.7 copy-start.3
  11.6 0.7 copy-start.4
  14.6 7.2 %copy-start.1 = (bf16[8,2048]{1,0:T(8,128)(2,1)}, bf16[8,2048]{1,0:T(8,128)(2,1)S(1)}, u32[]{:S(2)}) copy-start(bf16[8,2048]{1,0:T(8,128)(2,1)S(1)} %collective-permute-done.1.below) | copy-start | bytes 98308
  21.8 0.6 copy-start.2
